TPU v7x, 512 devices: a whole 4x8x8 slice. The times are simulated.
512 devices in a mesh: team: 16 (over y, core), tm: 32 (over x, z).
Axes of the slice: x: 4, y: 8, z: 8, core: 2. Of those that a mesh axis runs over, the one named last changes fastest.
Arguments:
- transitions: float32 [16, 32, 512, 512], P('team', 'tm'), may hold values from -0.25 to 1.25
- states: float32 [16, 32, 64, 512], P('team', 'tm'), may hold values from -1 to 1
- cotangent: float32 [16, 32, 64, 512], P('team', 'tm'), may hold values from -2.4 to 2.4
- terminal: float32 [16, 64, 512], P('team'), may hold values from -6 to 6
- incidence: int32 [16, 32, 32, 2048], P('team', 'tm'), may hold values 0 or 1
- measured: float32 [16, 32, 64, 32], P('team', 'tm'), may hold values from -0.12 to 0.12
- obs_gain: float32 [16, 512], P('team'), may hold values from -6 to 6
Outputs:
- adjoint: float32 [16, 32, 64, 512], P('team', 'tm')
- grad_transitions: bfloat16 [16, 32, 512, 512], P('team', 'tm')
All inputs are finite; a program needn't handle non-finite values. No bound on the sum of `incidence` on one device may be relied on, other than what follows from the above.
Results may differ from a plain program's by a relative error of at most 0.001.
Values sent between devices are 32-bit elements; how exact they have to be, the bound alone decides.
No kernel may reach another device: no remote copies, remote signals or barrier semaphores. Data moves between devices by JAX's collectives and lax.ppermute only.
A program may use at most 64 MiB of HBM per device.

v0:
```python
import jax
import jax.numpy as jnp
from jax import lax
from jax.sharding import PartitionSpec as P

STATES = 16
TEAM_STATES = 512
COLS = 64
HIGHEST = lax.Precision.HIGHEST


def from_behind(block, axis, distance):
    devices = range(lax.axis_size(axis))
    route = [(i - distance, i) for i in devices if i - distance in devices]
    return lax.ppermute(block, axis, route)


def matmul(left, right):
    return jnp.dot(left, right, precision=HIGHEST)


def shards(transitions, states, cotangent, terminal, incidence, measured, obs_gain):
    step_count = transitions.shape[1]
    matrices = transitions[0]
    incident = incidence[0].astype(jnp.float32)
    partial_value = jnp.einsum("scr,srl->scl", measured[0], incident, precision=HIGHEST)
    landmark = lax.psum(partial_value, "team")
    injection = jnp.einsum("scl,srl->scr", landmark, incident, precision=HIGHEST)
    driven = cotangent[0] + jnp.repeat(injection, STATES, axis=2) * obs_gain[0][None, None, :]
    offset = jnp.zeros((COLS, TEAM_STATES), jnp.float32)
    moment = 0
    offset = matmul(offset, matrices[moment]) + driven[moment]
    is_last = lax.axis_index("tm") == lax.axis_size("tm") - 1
    start_cot = jnp.where(is_last, terminal[0], jnp.zeros_like(terminal[0]))

    def advance_steps(turn, carried):
        outgoing = carried
        outgoing = matmul(outgoing, matrices[0])
        outgoing = outgoing + offset
        return from_behind(outgoing, "tm", -1) + start_cot

    incoming = lax.fori_loop(0, lax.axis_size("tm") - 1, advance_steps, start_cot)
    running = incoming
    adjoint_list = [None] * step_count
    grad_list = [None] * step_count
    moment = 0
    grad_now = jnp.einsum("cn,cm->nm", running, states[0, moment], precision=HIGHEST)
    grad_list[moment] = grad_now.astype(jnp.bfloat16)
    running = matmul(running, matrices[moment]) + driven[moment]
    adjoint_list[moment] = running
    adjoint = jnp.stack(adjoint_list)[None]
    grad_transitions = jnp.stack(grad_list)[None]
    return (adjoint, grad_transitions)


def solution(mesh):
    placed = (
        P("team", "tm", None, None),
        P("team", "tm", None, None),
        P("team", "tm", None, None),
        P("team", None, None),
        P("team", "tm", None, None),
        P("team", "tm", None, None),
        P("team", None),
    )
    return jax.shard_map(
        shards,
        mesh=mesh,
        in_specs=placed,
        out_specs=(P("team", "tm", None, None), P("team", "tm", None, None)),
        check_vma=False,
    )
```

profile of v0, /device:TPU:30, one launch (start us, length us, event | category | flops | bytes accessed | tf_op | source)
XLA Modules:
  0.0 454.6 jit_solution(4725242785528667431)
XLA Ops:
  10.6 120.1 %all-reduce.2.cloned.1.call-done = f32[64,2048]{1,0:T(8,128)} async-done(((f32[64,2048]{1,0:T(8,128)}), f32[64,2048]{1,0:T(8,128)}) %all-reduce.2.cloned.1.call-update) | async-done | bytes 524304 | tf_op jit(solution)/shard_map/psum | solution.py:27
  134.0 310.5 %while.10 = (s32[]{:T(128)}, f32[64,512]{1,0:T(8,128)S(1)}, f32[1,1,512,512]{3,2,1,0:T(8,128)S(1)}, f32[64,512]{1,0:T(8,128)S(1)}, f32[64,512]{1,0:T(8,128)S(1)}, /*index=5*/s32[]{:T(128)}) while((s32[]{:T(128)}, f32[64,512]{1,0:T(8,128)S(1)}, f32[1,1,512,512]{3,2,1,0:T(8,128)S(1)}, f32[64,512]{1,0:T(8,128)S(1)}, f32[64,512]{1,0:T(8,128)S(1)}, ...), condition=%wide.region_2.3_spmd, body=%wide.region_1.2_spmd.sunk | while | flops 201392128 | bytes 2359405 | solution.py:42
  145.5 6.5 %collective-permute-start = (f32[64,512]{1,0:T(8,128)S(1)}, f32[64,512]{1,0:T(8,128)S(1)}, u32[]{:S(2)}, u32[]{:S(2)}) collective-permute-start(f32[64,512]{1,0:T(8,128)S(1)} %convolution_add_fusion.4), channel_id=1, source_target_pairs={{1,0},{2,1},{3,2},{4,3},{5,4},{6,5},{7,6},{8,7},{9,8},{10,9},{11,1... | collective-permute-start | bytes 393224 | tf_op jit(solution)/shard_map/while/body/eval_jaxpr/ppermute | solution.py:15
  155.8 6.5 %collective-permute-start = (f32[64,512]{1,0:T(8,128)S(1)}, f32[64,512]{1,0:T(8,128)S(1)}, u32[]{:S(2)}, u32[]{:S(2)}) collective-permute-start(f32[64,512]{1,0:T(8,128)S(1)} %convolution_add_fusion.4), channel_id=1, source_target_pairs={{1,0},{2,1},{3,2},{4,3},{5,4},{6,5},{7,6},{8,7},{9,8},{10,9},{11,1... | collective-permute-start | bytes 393224 | tf_op jit(solution)/shard_map/while/body/eval_jaxpr/ppermute | solution.py:15
  165.6 6.5 %collective-permute-start = (f32[64,512]{1,0:T(8,128)S(1)}, f32[64,512]{1,0:T(8,128)S(1)}, u32[]{:S(2)}, u32[]{:S(2)}) collective-permute-start(f32[64,512]{1,0:T(8,128)S(1)} %convolution_add_fusion.4), channel_id=1, source_target_pairs={{1,0},{2,1},{3,2},{4,3},{5,4},{6,5},{7,6},{8,7},{9,8},{10,9},{11,1... | collective-permute-start | bytes 393224 | tf_op jit(solution)/shard_map/while/body/eval_jaxpr/ppermute | solution.py:15
  175.3 6.5 %collective-permute-start = (f32[64,512]{1,0:T(8,128)S(1)}, f32[64,512]{1,0:T(8,128)S(1)}, u32[]{:S(2)}, u32[]{:S(2)}) collective-permute-start(f32[64,512]{1,0:T(8,128)S(1)} %convolution_add_fusion.4), channel_id=1, source_target_pairs={{1,0},{2,1},{3,2},{4,3},{5,4},{6,5},{7,6},{8,7},{9,8},{10,9},{11,1... | collective-permute-start | bytes 393224 | tf_op jit(solution)/shard_map/while/body/eval_jaxpr/ppermute | solution.py:15
  185.1 6.5 %collective-permute-start = (f32[64,512]{1,0:T(8,128)S(1)}, f32[64,512]{1,0:T(8,128)S(1)}, u32[]{:S(2)}, u32[]{:S(2)}) collective-permute-start(f32[64,512]{1,0:T(8,128)S(1)} %convolution_add_fusion.4), channel_id=1, source_target_pairs={{1,0},{2,1},{3,2},{4,3},{5,4},{6,5},{7,6},{8,7},{9,8},{10,9},{11,1... | collective-permute-start | bytes 393224 | tf_op jit(solution)/shard_map/while/body/eval_jaxpr/ppermute | solution.py:15
  194.8 6.5 %collective-permute-start = (f32[64,512]{1,0:T(8,128)S(1)}, f32[64,512]{1,0:T(8,128)S(1)}, u32[]{:S(2)}, u32[]{:S(2)}) collective-permute-start(f32[64,512]{1,0:T(8,128)S(1)} %convolution_add_fusion.4), channel_id=1, source_target_pairs={{1,0},{2,1},{3,2},{4,3},{5,4},{6,5},{7,6},{8,7},{9,8},{10,9},{11,1... | collective-permute-start | bytes 393224 | tf_op jit(solution)/shard_map/while/body/eval_jaxpr/ppermute | solution.py:15
  204.6 6.5 %collective-permute-start = (f32[64,512]{1,0:T(8,128)S(1)}, f32[64,512]{1,0:T(8,128)S(1)}, u32[]{:S(2)}, u32[]{:S(2)}) collective-permute-start(f32[64,512]{1,0:T(8,128)S(1)} %convolution_add_fusion.4), channel_id=1, source_target_pairs={{1,0},{2,1},{3,2},{4,3},{5,4},{6,5},{7,6},{8,7},{9,8},{10,9},{11,1... | collective-permute-start | bytes 393224 | tf_op jit(solution)/shard_map/while/body/eval_jaxpr/ppermute | solution.py:15
  214.6 6.5 %collective-permute-start = (f32[64,512]{1,0:T(8,128)S(1)}, f32[64,512]{1,0:T(8,128)S(1)}, u32[]{:S(2)}, u32[]{:S(2)}) collective-permute-start(f32[64,512]{1,0:T(8,128)S(1)} %convolution_add_fusion.4), channel_id=1, source_target_pairs={{1,0},{2,1},{3,2},{4,3},{5,4},{6,5},{7,6},{8,7},{9,8},{10,9},{11,1... | collective-permute-start | bytes 393224 | tf_op jit(solution)/shard_map/while/body/eval_jaxpr/ppermute | solution.py:15
  225.8 6.5 %collective-permute-start = (f32[64,512]{1,0:T(8,128)S(1)}, f32[64,512]{1,0:T(8,128)S(1)}, u32[]{:S(2)}, u32[]{:S(2)}) collective-permute-start(f32[64,512]{1,0:T(8,128)S(1)} %convolution_add_fusion.4), channel_id=1, source_target_pairs={{1,0},{2,1},{3,2},{4,3},{5,4},{6,5},{7,6},{8,7},{9,8},{10,9},{11,1... | collective-permute-start | bytes 393224 | tf_op jit(solution)/shard_map/while/body/eval_jaxpr/ppermute | solution.py:15
  236.0 6.5 %collective-permute-start = (f32[64,512]{1,0:T(8,128)S(1)}, f32[64,512]{1,0:T(8,128)S(1)}, u32[]{:S(2)}, u32[]{:S(2)}) collective-permute-start(f32[64,512]{1,0:T(8,128)S(1)} %convolution_add_fusion.4), channel_id=1, source_target_pairs={{1,0},{2,1},{3,2},{4,3},{5,4},{6,5},{7,6},{8,7},{9,8},{10,9},{11,1... | collective-permute-start | bytes 393224 | tf_op jit(solution)/shard_map/while/body/eval_jaxpr/ppermute | solution.py:15
  245.8 6.5 %collective-permute-start = (f32[64,512]{1,0:T(8,128)S(1)}, f32[64,512]{1,0:T(8,128)S(1)}, u32[]{:S(2)}, u32[]{:S(2)}) collective-permute-start(f32[64,512]{1,0:T(8,128)S(1)} %convolution_add_fusion.4), channel_id=1, source_target_pairs={{1,0},{2,1},{3,2},{4,3},{5,4},{6,5},{7,6},{8,7},{9,8},{10,9},{11,1... | collective-permute-start | bytes 393224 | tf_op jit(solution)/shard_map/while/body/eval_jaxpr/ppermute | solution.py:15
  255.5 6.5 %collective-permute-start = (f32[64,512]{1,0:T(8,128)S(1)}, f32[64,512]{1,0:T(8,128)S(1)}, u32[]{:S(2)}, u32[]{:S(2)}) collective-permute-start(f32[64,512]{1,0:T(8,128)S(1)} %convolution_add_fusion.4), channel_id=1, source_target_pairs={{1,0},{2,1},{3,2},{4,3},{5,4},{6,5},{7,6},{8,7},{9,8},{10,9},{11,1... | collective-permute-start | bytes 393224 | tf_op jit(solution)/shard_map/while/body/eval_jaxpr/ppermute | solution.py:15
  265.3 6.5 %collective-permute-start = (f32[64,512]{1,0:T(8,128)S(1)}, f32[64,512]{1,0:T(8,128)S(1)}, u32[]{:S(2)}, u32[]{:S(2)}) collective-permute-start(f32[64,512]{1,0:T(8,128)S(1)} %convolution_add_fusion.4), channel_id=1, source_target_pairs={{1,0},{2,1},{3,2},{4,3},{5,4},{6,5},{7,6},{8,7},{9,8},{10,9},{11,1... | collective-permute-start | bytes 393224 | tf_op jit(solution)/shard_map/while/body/eval_jaxpr/ppermute | solution.py:15
  275.1 6.5 %collective-permute-start = (f32[64,512]{1,0:T(8,128)S(1)}, f32[64,512]{1,0:T(8,128)S(1)}, u32[]{:S(2)}, u32[]{:S(2)}) collective-permute-start(f32[64,512]{1,0:T(8,128)S(1)} %convolution_add_fusion.4), channel_id=1, source_target_pairs={{1,0},{2,1},{3,2},{4,3},{5,4},{6,5},{7,6},{8,7},{9,8},{10,9},{11,1... | collective-permute-start | bytes 393224 | tf_op jit(solution)/shard_map/while/body/eval_jaxpr/ppermute | solution.py:15
  284.8 6.5 %collective-permute-start = (f32[64,512]{1,0:T(8,128)S(1)}, f32[64,512]{1,0:T(8,128)S(1)}, u32[]{:S(2)}, u32[]{:S(2)}) collective-permute-start(f32[64,512]{1,0:T(8,128)S(1)} %convolution_add_fusion.4), channel_id=1, source_target_pairs={{1,0},{2,1},{3,2},{4,3},{5,4},{6,5},{7,6},{8,7},{9,8},{10,9},{11,1... | collective-permute-start | bytes 393224 | tf_op jit(solution)/shard_map/while/body/eval_jaxpr/ppermute | solution.py:15
  294.8 6.5 %collective-permute-start = (f32[64,512]{1,0:T(8,128)S(1)}, f32[64,512]{1,0:T(8,128)S(1)}, u32[]{:S(2)}, u32[]{:S(2)}) collective-permute-start(f32[64,512]{1,0:T(8,128)S(1)} %convolution_add_fusion.4), channel_id=1, source_target_pairs={{1,0},{2,1},{3,2},{4,3},{5,4},{6,5},{7,6},{8,7},{9,8},{10,9},{11,1... | collective-permute-start | bytes 393224 | tf_op jit(solution)/shard_map/while/body/eval_jaxpr/ppermute | solution.py:15
  306.0 6.5 %collective-permute-start = (f32[64,512]{1,0:T(8,128)S(1)}, f32[64,512]{1,0:T(8,128)S(1)}, u32[]{:S(2)}, u32[]{:S(2)}) collective-permute-start(f32[64,512]{1,0:T(8,128)S(1)} %convolution_add_fusion.4), channel_id=1, source_target_pairs={{1,0},{2,1},{3,2},{4,3},{5,4},{6,5},{7,6},{8,7},{9,8},{10,9},{11,1... | collective-permute-start | bytes 393224 | tf_op jit(solution)/shard_map/while/body/eval_jaxpr/ppermute | solution.py:15
  316.2 6.5 %collective-permute-start = (f32[64,512]{1,0:T(8,128)S(1)}, f32[64,512]{1,0:T(8,128)S(1)}, u32[]{:S(2)}, u32[]{:S(2)}) collective-permute-start(f32[64,512]{1,0:T(8,128)S(1)} %convolution_add_fusion.4), channel_id=1, source_target_pairs={{1,0},{2,1},{3,2},{4,3},{5,4},{6,5},{7,6},{8,7},{9,8},{10,9},{11,1... | collective-permute-start | bytes 393224 | tf_op jit(solution)/shard_map/while/body/eval_jaxpr/ppermute | solution.py:15
  326.0 6.5 %collective-permute-start = (f32[64,512]{1,0:T(8,128)S(1)}, f32[64,512]{1,0:T(8,128)S(1)}, u32[]{:S(2)}, u32[]{:S(2)}) collective-permute-start(f32[64,512]{1,0:T(8,128)S(1)} %convolution_add_fusion.4), channel_id=1, source_target_pairs={{1,0},{2,1},{3,2},{4,3},{5,4},{6,5},{7,6},{8,7},{9,8},{10,9},{11,1... | collective-permute-start | bytes 393224 | tf_op jit(solution)/shard_map/while/body/eval_jaxpr/ppermute | solution.py:15
  335.8 6.5 %collective-permute-start = (f32[64,512]{1,0:T(8,128)S(1)}, f32[64,512]{1,0:T(8,128)S(1)}, u32[]{:S(2)}, u32[]{:S(2)}) collective-permute-start(f32[64,512]{1,0:T(8,128)S(1)} %convolution_add_fusion.4), channel_id=1, source_target_pairs={{1,0},{2,1},{3,2},{4,3},{5,4},{6,5},{7,6},{8,7},{9,8},{10,9},{11,1... | collective-permute-start | bytes 393224 | tf_op jit(solution)/shard_map/while/body/eval_jaxpr/ppermute | solution.py:15
  345.5 6.5 %collective-permute-start = (f32[64,512]{1,0:T(8,128)S(1)}, f32[64,512]{1,0:T(8,128)S(1)}, u32[]{:S(2)}, u32[]{:S(2)}) collective-permute-start(f32[64,512]{1,0:T(8,128)S(1)} %convolution_add_fusion.4), channel_id=1, source_target_pairs={{1,0},{2,1},{3,2},{4,3},{5,4},{6,5},{7,6},{8,7},{9,8},{10,9},{11,1... | collective-permute-start | bytes 393224 | tf_op jit(solution)/shard_map/while/body/eval_jaxpr/ppermute | solution.py:15
  355.3 6.5 %collective-permute-start = (f32[64,512]{1,0:T(8,128)S(1)}, f32[64,512]{1,0:T(8,128)S(1)}, u32[]{:S(2)}, u32[]{:S(2)}) collective-permute-start(f32[64,512]{1,0:T(8,128)S(1)} %convolution_add_fusion.4), channel_id=1, source_target_pairs={{1,0},{2,1},{3,2},{4,3},{5,4},{6,5},{7,6},{8,7},{9,8},{10,9},{11,1... | collective-permute-start | bytes 393224 | tf_op jit(solution)/shard_map/while/body/eval_jaxpr/ppermute | solution.py:15
  365.0 6.5 %collective-permute-start = (f32[64,512]{1,0:T(8,128)S(1)}, f32[64,512]{1,0:T(8,128)S(1)}, u32[]{:S(2)}, u32[]{:S(2)}) collective-permute-start(f32[64,512]{1,0:T(8,128)S(1)} %convolution_add_fusion.4), channel_id=1, source_target_pairs={{1,0},{2,1},{3,2},{4,3},{5,4},{6,5},{7,6},{8,7},{9,8},{10,9},{11,1... | collective-permute-start | bytes 393224 | tf_op jit(solution)/shard_map/while/body/eval_jaxpr/ppermute | solution.py:15
  375.1 6.5 %collective-permute-start = (f32[64,512]{1,0:T(8,128)S(1)}, f32[64,512]{1,0:T(8,128)S(1)}, u32[]{:S(2)}, u32[]{:S(2)}) collective-permute-start(f32[64,512]{1,0:T(8,128)S(1)} %convolution_add_fusion.4), channel_id=1, source_target_pairs={{1,0},{2,1},{3,2},{4,3},{5,4},{6,5},{7,6},{8,7},{9,8},{10,9},{11,1... | collective-permute-start | bytes 393224 | tf_op jit(solution)/shard_map/while/body/eval_jaxpr/ppermute | solution.py:15
  386.2 6.5 %collective-permute-start = (f32[64,512]{1,0:T(8,128)S(1)}, f32[64,512]{1,0:T(8,128)S(1)}, u32[]{:S(2)}, u32[]{:S(2)}) collective-permute-start(f32[64,512]{1,0:T(8,128)S(1)} %convolution_add_fusion.4), channel_id=1, source_target_pairs={{1,0},{2,1},{3,2},{4,3},{5,4},{6,5},{7,6},{8,7},{9,8},{10,9},{11,1... | collective-permute-start | bytes 393224 | tf_op jit(solution)/shard_map/while/body/eval_jaxpr/ppermute | solution.py:15
  396.4 6.5 %collective-permute-start = (f32[64,512]{1,0:T(8,128)S(1)}, f32[64,512]{1,0:T(8,128)S(1)}, u32[]{:S(2)}, u32[]{:S(2)}) collective-permute-start(f32[64,512]{1,0:T(8,128)S(1)} %convolution_add_fusion.4), channel_id=1, source_target_pairs={{1,0},{2,1},{3,2},{4,3},{5,4},{6,5},{7,6},{8,7},{9,8},{10,9},{11,1... | collective-permute-start | bytes 393224 | tf_op jit(solution)/shard_map/while/body/eval_jaxpr/ppermute | solution.py:15
  406.2 6.5 %collective-permute-start = (f32[64,512]{1,0:T(8,128)S(1)}, f32[64,512]{1,0:T(8,128)S(1)}, u32[]{:S(2)}, u32[]{:S(2)}) collective-permute-start(f32[64,512]{1,0:T(8,128)S(1)} %convolution_add_fusion.4), channel_id=1, source_target_pairs={{1,0},{2,1},{3,2},{4,3},{5,4},{6,5},{7,6},{8,7},{9,8},{10,9},{11,1... | collective-permute-start | bytes 393224 | tf_op jit(solution)/shard_map/while/body/eval_jaxpr/ppermute | solution.py:15
  416.0 6.5 %collective-permute-start = (f32[64,512]{1,0:T(8,128)S(1)}, f32[64,512]{1,0:T(8,128)S(1)}, u32[]{:S(2)}, u32[]{:S(2)}) collective-permute-start(f32[64,512]{1,0:T(8,128)S(1)} %convolution_add_fusion.4), channel_id=1, source_target_pairs={{1,0},{2,1},{3,2},{4,3},{5,4},{6,5},{7,6},{8,7},{9,8},{10,9},{11,1... | collective-permute-start | bytes 393224 | tf_op jit(solution)/shard_map/while/body/eval_jaxpr/ppermute | solution.py:15
  425.8 6.5 %collective-permute-start = (f32[64,512]{1,0:T(8,128)S(1)}, f32[64,512]{1,0:T(8,128)S(1)}, u32[]{:S(2)}, u32[]{:S(2)}) collective-permute-start(f32[64,512]{1,0:T(8,128)S(1)} %convolution_add_fusion.4), channel_id=1, source_target_pairs={{1,0},{2,1},{3,2},{4,3},{5,4},{6,5},{7,6},{8,7},{9,8},{10,9},{11,1... | collective-permute-start | bytes 393224 | tf_op jit(solution)/shard_map/while/body/eval_jaxpr/ppermute | solution.py:15
  435.5 6.5 %collective-permute-start = (f32[64,512]{1,0:T(8,128)S(1)}, f32[64,512]{1,0:T(8,128)S(1)}, u32[]{:S(2)}, u32[]{:S(2)}) collective-permute-start(f32[64,512]{1,0:T(8,128)S(1)} %convolution_add_fusion.4), channel_id=1, source_target_pairs={{1,0},{2,1},{3,2},{4,3},{5,4},{6,5},{7,6},{8,7},{9,8},{10,9},{11,1... | collective-permute-start | bytes 393224 | tf_op jit(solution)/shard_map/while/body/eval_jaxpr/ppermute | solution.py:15
  (117 shorter events, 125.4 us)
Async XLA Ops:
  7.2 123.5 %all-reduce.2.cloned.1.call-start = ((), (), s32[]{:S(2)}) async-start(), calls=%async_computation | async-start | bytes 1048576 | tf_op jit(solution)/shard_map/psum | solution.py:27
  134.8 10.0 %collective-permute-start = (f32[64,512]{1,0:T(8,128)S(1)}, f32[64,512]{1,0:T(8,128)S(1)}, u32[]{:S(2)}, u32[]{:S(2)}) collective-permute-start(f32[64,512]{1,0:T(8,128)S(1)} %convolution_add_fusion.4), channel_id=1, source_target_pairs={{1,0},{2,1},{3,2},{4,3},{5,4},{6,5},{7,6},{8,7},{9,8},{10,9},{11,1... | collective-permute-start | bytes 393224 | tf_op jit(solution)/shard_map/while/body/eval_jaxpr/ppermute | solution.py:15
  145.5 9.4 %collective-permute-start = (f32[64,512]{1,0:T(8,128)S(1)}, f32[64,512]{1,0:T(8,128)S(1)}, u32[]{:S(2)}, u32[]{:S(2)}) collective-permute-start(f32[64,512]{1,0:T(8,128)S(1)} %convolution_add_fusion.4), channel_id=1, source_target_pairs={{1,0},{2,1},{3,2},{4,3},{5,4},{6,5},{7,6},{8,7},{9,8},{10,9},{11,1... | collective-permute-start | bytes 393224 | tf_op jit(solution)/shard_map/while/body/eval_jaxpr/ppermute | solution.py:15
  155.8 9.0 %collective-permute-start = (f32[64,512]{1,0:T(8,128)S(1)}, f32[64,512]{1,0:T(8,128)S(1)}, u32[]{:S(2)}, u32[]{:S(2)}) collective-permute-start(f32[64,512]{1,0:T(8,128)S(1)} %convolution_add_fusion.4), channel_id=1, source_target_pairs={{1,0},{2,1},{3,2},{4,3},{5,4},{6,5},{7,6},{8,7},{9,8},{10,9},{11,1... | collective-permute-start | bytes 393224 | tf_op jit(solution)/shard_map/while/body/eval_jaxpr/ppermute | solution.py:15
  165.6 9.0 %collective-permute-start = (f32[64,512]{1,0:T(8,128)S(1)}, f32[64,512]{1,0:T(8,128)S(1)}, u32[]{:S(2)}, u32[]{:S(2)}) collective-permute-start(f32[64,512]{1,0:T(8,128)S(1)} %convolution_add_fusion.4), channel_id=1, source_target_pairs={{1,0},{2,1},{3,2},{4,3},{5,4},{6,5},{7,6},{8,7},{9,8},{10,9},{11,1... | collective-permute-start | bytes 393224 | tf_op jit(solution)/shard_map/while/body/eval_jaxpr/ppermute | solution.py:15
  175.3 9.0 %collective-permute-start = (f32[64,512]{1,0:T(8,128)S(1)}, f32[64,512]{1,0:T(8,128)S(1)}, u32[]{:S(2)}, u32[]{:S(2)}) collective-permute-start(f32[64,512]{1,0:T(8,128)S(1)} %convolution_add_fusion.4), channel_id=1, source_target_pairs={{1,0},{2,1},{3,2},{4,3},{5,4},{6,5},{7,6},{8,7},{9,8},{10,9},{11,1... | collective-permute-start | bytes 393224 | tf_op jit(solution)/shard_map/while/body/eval_jaxpr/ppermute | solution.py:15
  185.1 9.0 %collective-permute-start = (f32[64,512]{1,0:T(8,128)S(1)}, f32[64,512]{1,0:T(8,128)S(1)}, u32[]{:S(2)}, u32[]{:S(2)}) collective-permute-start(f32[64,512]{1,0:T(8,128)S(1)} %convolution_add_fusion.4), channel_id=1, source_target_pairs={{1,0},{2,1},{3,2},{4,3},{5,4},{6,5},{7,6},{8,7},{9,8},{10,9},{11,1... | collective-permute-start | bytes 393224 | tf_op jit(solution)/shard_map/while/body/eval_jaxpr/ppermute | solution.py:15
  194.8 9.0 %collective-permute-start = (f32[64,512]{1,0:T(8,128)S(1)}, f32[64,512]{1,0:T(8,128)S(1)}, u32[]{:S(2)}, u32[]{:S(2)}) collective-permute-start(f32[64,512]{1,0:T(8,128)S(1)} %convolution_add_fusion.4), channel_id=1, source_target_pairs={{1,0},{2,1},{3,2},{4,3},{5,4},{6,5},{7,6},{8,7},{9,8},{10,9},{11,1... | collective-permute-start | bytes 393224 | tf_op jit(solution)/shard_map/while/body/eval_jaxpr/ppermute | solution.py:15
  204.6 9.2 %collective-permute-start = (f32[64,512]{1,0:T(8,128)S(1)}, f32[64,512]{1,0:T(8,128)S(1)}, u32[]{:S(2)}, u32[]{:S(2)}) collective-permute-start(f32[64,512]{1,0:T(8,128)S(1)} %convolution_add_fusion.4), channel_id=1, source_target_pairs={{1,0},{2,1},{3,2},{4,3},{5,4},{6,5},{7,6},{8,7},{9,8},{10,9},{11,1... | collective-permute-start | bytes 393224 | tf_op jit(solution)/shard_map/while/body/eval_jaxpr/ppermute | solution.py:15
  214.6 10.4 %collective-permute-start = (f32[64,512]{1,0:T(8,128)S(1)}, f32[64,512]{1,0:T(8,128)S(1)}, u32[]{:S(2)}, u32[]{:S(2)}) collective-permute-start(f32[64,512]{1,0:T(8,128)S(1)} %convolution_add_fusion.4), channel_id=1, source_target_pairs={{1,0},{2,1},{3,2},{4,3},{5,4},{6,5},{7,6},{8,7},{9,8},{10,9},{11,1... | collective-permute-start | bytes 393224 | tf_op jit(solution)/shard_map/while/body/eval_jaxpr/ppermute | solution.py:15
  225.8 9.4 %collective-permute-start = (f32[64,512]{1,0:T(8,128)S(1)}, f32[64,512]{1,0:T(8,128)S(1)}, u32[]{:S(2)}, u32[]{:S(2)}) collective-permute-start(f32[64,512]{1,0:T(8,128)S(1)} %convolution_add_fusion.4), channel_id=1, source_target_pairs={{1,0},{2,1},{3,2},{4,3},{5,4},{6,5},{7,6},{8,7},{9,8},{10,9},{11,1... | collective-permute-start | bytes 393224 | tf_op jit(solution)/shard_map/while/body/eval_jaxpr/ppermute | solution.py:15
  236.0 9.0 %collective-permute-start = (f32[64,512]{1,0:T(8,128)S(1)}, f32[64,512]{1,0:T(8,128)S(1)}, u32[]{:S(2)}, u32[]{:S(2)}) collective-permute-start(f32[64,512]{1,0:T(8,128)S(1)} %convolution_add_fusion.4), channel_id=1, source_target_pairs={{1,0},{2,1},{3,2},{4,3},{5,4},{6,5},{7,6},{8,7},{9,8},{10,9},{11,1... | collective-permute-start | bytes 393224 | tf_op jit(solution)/shard_map/while/body/eval_jaxpr/ppermute | solution.py:15
  245.8 9.0 %collective-permute-start = (f32[64,512]{1,0:T(8,128)S(1)}, f32[64,512]{1,0:T(8,128)S(1)}, u32[]{:S(2)}, u32[]{:S(2)}) collective-permute-start(f32[64,512]{1,0:T(8,128)S(1)} %convolution_add_fusion.4), channel_id=1, source_target_pairs={{1,0},{2,1},{3,2},{4,3},{5,4},{6,5},{7,6},{8,7},{9,8},{10,9},{11,1... | collective-permute-start | bytes 393224 | tf_op jit(solution)/shard_map/while/body/eval_jaxpr/ppermute | solution.py:15
  255.5 9.0 %collective-permute-start = (f32[64,512]{1,0:T(8,128)S(1)}, f32[64,512]{1,0:T(8,128)S(1)}, u32[]{:S(2)}, u32[]{:S(2)}) collective-permute-start(f32[64,512]{1,0:T(8,128)S(1)} %convolution_add_fusion.4), channel_id=1, source_target_pairs={{1,0},{2,1},{3,2},{4,3},{5,4},{6,5},{7,6},{8,7},{9,8},{10,9},{11,1... | collective-permute-start | bytes 393224 | tf_op jit(solution)/shard_map/while/body/eval_jaxpr/ppermute | solution.py:15
  265.3 9.0 %collective-permute-start = (f32[64,512]{1,0:T(8,128)S(1)}, f32[64,512]{1,0:T(8,128)S(1)}, u32[]{:S(2)}, u32[]{:S(2)}) collective-permute-start(f32[64,512]{1,0:T(8,128)S(1)} %convolution_add_fusion.4), channel_id=1, source_target_pairs={{1,0},{2,1},{3,2},{4,3},{5,4},{6,5},{7,6},{8,7},{9,8},{10,9},{11,1... | collective-permute-start | bytes 393224 | tf_op jit(solution)/shard_map/while/body/eval_jaxpr/ppermute | solution.py:15
  275.1 9.0 %collective-permute-start = (f32[64,512]{1,0:T(8,128)S(1)}, f32[64,512]{1,0:T(8,128)S(1)}, u32[]{:S(2)}, u32[]{:S(2)}) collective-permute-start(f32[64,512]{1,0:T(8,128)S(1)} %convolution_add_fusion.4), channel_id=1, source_target_pairs={{1,0},{2,1},{3,2},{4,3},{5,4},{6,5},{7,6},{8,7},{9,8},{10,9},{11,1... | collective-permute-start | bytes 393224 | tf_op jit(solution)/shard_map/while/body/eval_jaxpr/ppermute | solution.py:15
  284.8 9.2 %collective-permute-start = (f32[64,512]{1,0:T(8,128)S(1)}, f32[64,512]{1,0:T(8,128)S(1)}, u32[]{:S(2)}, u32[]{:S(2)}) collective-permute-start(f32[64,512]{1,0:T(8,128)S(1)} %convolution_add_fusion.4), channel_id=1, source_target_pairs={{1,0},{2,1},{3,2},{4,3},{5,4},{6,5},{7,6},{8,7},{9,8},{10,9},{11,1... | collective-permute-start | bytes 393224 | tf_op jit(solution)/shard_map/while/body/eval_jaxpr/ppermute | solution.py:15
  294.8 10.3 %collective-permute-start = (f32[64,512]{1,0:T(8,128)S(1)}, f32[64,512]{1,0:T(8,128)S(1)}, u32[]{:S(2)}, u32[]{:S(2)}) collective-permute-start(f32[64,512]{1,0:T(8,128)S(1)} %convolution_add_fusion.4), channel_id=1, source_target_pairs={{1,0},{2,1},{3,2},{4,3},{5,4},{6,5},{7,6},{8,7},{9,8},{10,9},{11,1... | collective-permute-start | bytes 393224 | tf_op jit(solution)/shard_map/while/body/eval_jaxpr/ppermute | solution.py:15
  306.0 9.5 %collective-permute-start = (f32[64,512]{1,0:T(8,128)S(1)}, f32[64,512]{1,0:T(8,128)S(1)}, u32[]{:S(2)}, u32[]{:S(2)}) collective-permute-start(f32[64,512]{1,0:T(8,128)S(1)} %convolution_add_fusion.4), channel_id=1, source_target_pairs={{1,0},{2,1},{3,2},{4,3},{5,4},{6,5},{7,6},{8,7},{9,8},{10,9},{11,1... | collective-permute-start | bytes 393224 | tf_op jit(solution)/shard_map/while/body/eval_jaxpr/ppermute | solution.py:15
  316.2 9.0 %collective-permute-start = (f32[64,512]{1,0:T(8,128)S(1)}, f32[64,512]{1,0:T(8,128)S(1)}, u32[]{:S(2)}, u32[]{:S(2)}) collective-permute-start(f32[64,512]{1,0:T(8,128)S(1)} %convolution_add_fusion.4), channel_id=1, source_target_pairs={{1,0},{2,1},{3,2},{4,3},{5,4},{6,5},{7,6},{8,7},{9,8},{10,9},{11,1... | collective-permute-start | bytes 393224 | tf_op jit(solution)/shard_map/while/body/eval_jaxpr/ppermute | solution.py:15
  326.0 9.0 %collective-permute-start = (f32[64,512]{1,0:T(8,128)S(1)}, f32[64,512]{1,0:T(8,128)S(1)}, u32[]{:S(2)}, u32[]{:S(2)}) collective-permute-start(f32[64,512]{1,0:T(8,128)S(1)} %convolution_add_fusion.4), channel_id=1, source_target_pairs={{1,0},{2,1},{3,2},{4,3},{5,4},{6,5},{7,6},{8,7},{9,8},{10,9},{11,1... | collective-permute-start | bytes 393224 | tf_op jit(solution)/shard_map/while/body/eval_jaxpr/ppermute | solution.py:15
  335.8 9.0 %collective-permute-start = (f32[64,512]{1,0:T(8,128)S(1)}, f32[64,512]{1,0:T(8,128)S(1)}, u32[]{:S(2)}, u32[]{:S(2)}) collective-permute-start(f32[64,512]{1,0:T(8,128)S(1)} %convolution_add_fusion.4), channel_id=1, source_target_pairs={{1,0},{2,1},{3,2},{4,3},{5,4},{6,5},{7,6},{8,7},{9,8},{10,9},{11,1... | collective-permute-start | bytes 393224 | tf_op jit(solution)/shard_map/while/body/eval_jaxpr/ppermute | solution.py:15
  345.5 9.0 %collective-permute-start = (f32[64,512]{1,0:T(8,128)S(1)}, f32[64,512]{1,0:T(8,128)S(1)}, u32[]{:S(2)}, u32[]{:S(2)}) collective-permute-start(f32[64,512]{1,0:T(8,128)S(1)} %convolution_add_fusion.4), channel_id=1, source_target_pairs={{1,0},{2,1},{3,2},{4,3},{5,4},{6,5},{7,6},{8,7},{9,8},{10,9},{11,1... | collective-permute-start | bytes 393224 | tf_op jit(solution)/shard_map/while/body/eval_jaxpr/ppermute | solution.py:15
  355.3 9.0 %collective-permute-start = (f32[64,512]{1,0:T(8,128)S(1)}, f32[64,512]{1,0:T(8,128)S(1)}, u32[]{:S(2)}, u32[]{:S(2)}) collective-permute-start(f32[64,512]{1,0:T(8,128)S(1)} %convolution_add_fusion.4), channel_id=1, source_target_pairs={{1,0},{2,1},{3,2},{4,3},{5,4},{6,5},{7,6},{8,7},{9,8},{10,9},{11,1... | collective-permute-start | bytes 393224 | tf_op jit(solution)/shard_map/while/body/eval_jaxpr/ppermute | solution.py:15
  365.0 9.2 %collective-permute-start = (f32[64,512]{1,0:T(8,128)S(1)}, f32[64,512]{1,0:T(8,128)S(1)}, u32[]{:S(2)}, u32[]{:S(2)}) collective-permute-start(f32[64,512]{1,0:T(8,128)S(1)} %convolution_add_fusion.4), channel_id=1, source_target_pairs={{1,0},{2,1},{3,2},{4,3},{5,4},{6,5},{7,6},{8,7},{9,8},{10,9},{11,1... | collective-permute-start | bytes 393224 | tf_op jit(solution)/shard_map/while/body/eval_jaxpr/ppermute | solution.py:15
  375.1 10.4 %collective-permute-start = (f32[64,512]{1,0:T(8,128)S(1)}, f32[64,512]{1,0:T(8,128)S(1)}, u32[]{:S(2)}, u32[]{:S(2)}) collective-permute-start(f32[64,512]{1,0:T(8,128)S(1)} %convolution_add_fusion.4), channel_id=1, source_target_pairs={{1,0},{2,1},{3,2},{4,3},{5,4},{6,5},{7,6},{8,7},{9,8},{10,9},{11,1... | collective-permute-start | bytes 393224 | tf_op jit(solution)/shard_map/while/body/eval_jaxpr/ppermute | solution.py:15
  386.2 9.4 %collective-permute-start = (f32[64,512]{1,0:T(8,128)S(1)}, f32[64,512]{1,0:T(8,128)S(1)}, u32[]{:S(2)}, u32[]{:S(2)}) collective-permute-start(f32[64,512]{1,0:T(8,128)S(1)} %convolution_add_fusion.4), channel_id=1, source_target_pairs={{1,0},{2,1},{3,2},{4,3},{5,4},{6,5},{7,6},{8,7},{9,8},{10,9},{11,1... | collective-permute-start | bytes 393224 | tf_op jit(solution)/shard_map/while/body/eval_jaxpr/ppermute | solution.py:15
  396.4 9.0 %collective-permute-start = (f32[64,512]{1,0:T(8,128)S(1)}, f32[64,512]{1,0:T(8,128)S(1)}, u32[]{:S(2)}, u32[]{:S(2)}) collective-permute-start(f32[64,512]{1,0:T(8,128)S(1)} %convolution_add_fusion.4), channel_id=1, source_target_pairs={{1,0},{2,1},{3,2},{4,3},{5,4},{6,5},{7,6},{8,7},{9,8},{10,9},{11,1... | collective-permute-start | bytes 393224 | tf_op jit(solution)/shard_map/while/body/eval_jaxpr/ppermute | solution.py:15
  406.2 9.0 %collective-permute-start = (f32[64,512]{1,0:T(8,128)S(1)}, f32[64,512]{1,0:T(8,128)S(1)}, u32[]{:S(2)}, u32[]{:S(2)}) collective-permute-start(f32[64,512]{1,0:T(8,128)S(1)} %convolution_add_fusion.4), channel_id=1, source_target_pairs={{1,0},{2,1},{3,2},{4,3},{5,4},{6,5},{7,6},{8,7},{9,8},{10,9},{11,1... | collective-permute-start | bytes 393224 | tf_op jit(solution)/shard_map/while/body/eval_jaxpr/ppermute | solution.py:15
  416.0 9.0 %collective-permute-start = (f32[64,512]{1,0:T(8,128)S(1)}, f32[64,512]{1,0:T(8,128)S(1)}, u32[]{:S(2)}, u32[]{:S(2)}) collective-permute-start(f32[64,512]{1,0:T(8,128)S(1)} %convolution_add_fusion.4), channel_id=1, source_target_pairs={{1,0},{2,1},{3,2},{4,3},{5,4},{6,5},{7,6},{8,7},{9,8},{10,9},{11,1... | collective-permute-start | bytes 393224 | tf_op jit(solution)/shard_map/while/body/eval_jaxpr/ppermute | solution.py:15
  425.8 9.0 %collective-permute-start = (f32[64,512]{1,0:T(8,128)S(1)}, f32[64,512]{1,0:T(8,128)S(1)}, u32[]{:S(2)}, u32[]{:S(2)}) collective-permute-start(f32[64,512]{1,0:T(8,128)S(1)} %convolution_add_fusion.4), channel_id=1, source_target_pairs={{1,0},{2,1},{3,2},{4,3},{5,4},{6,5},{7,6},{8,7},{9,8},{10,9},{11,1... | collective-permute-start | bytes 393224 | tf_op jit(solution)/shard_map/while/body/eval_jaxpr/ppermute | solution.py:15
  435.5 9.0 %collective-permute-start = (f32[64,512]{1,0:T(8,128)S(1)}, f32[64,512]{1,0:T(8,128)S(1)}, u32[]{:S(2)}, u32[]{:S(2)}) collective-permute-start(f32[64,512]{1,0:T(8,128)S(1)} %convolution_add_fusion.4), channel_id=1, source_target_pairs={{1,0},{2,1},{3,2},{4,3},{5,4},{6,5},{7,6},{8,7},{9,8},{10,9},{11,1... | collective-permute-start | bytes 393224 | tf_op jit(solution)/shard_map/while/body/eval_jaxpr/ppermute | solution.py:15
  (6 other events, 685.4 us)
Sparse Core Ops, SparseCore 0:
  10.9 119.8 all-reduce.1
where the time goes:
time: 456 us; the launch traced here: 455 us
  waiting for transfers between devices  206 us (45%)
  starting transfers between devices  200 us (44%)
  matrix products  31.3 us (7%)
  between operations  14.1 us (3%)
    ppermute x31, starting transfers between devices, from_behind(): return lax.ppermute(block, axis, route)  200 us
    psum x1, waiting for transfers between devices, shards(): landmark = lax.psum(partial_value, 'team')  120 us
    ppermute x31, waiting for transfers between devices, from_behind(): return lax.ppermute(block, axis, route)  85.5 us
    dot_general x33, matrix products, matmul(): return jnp.dot(left, right, precision=HIGHEST)  25.5 us
  transfers between devices with their start and end apart: 32, of which 32 were waited for; matrix products, arithmetic and copies ran while one was open for 0% of the time, Pallas kernels for 0%

commit v1 on v0

--- a/solution.py
+++ b/solution.py
@@ -24,7 +24,10 @@
     matrices = transitions[0]
     incident = incidence[0].astype(jnp.float32)
     partial_value = jnp.einsum("scr,srl->scl", measured[0], incident, precision=HIGHEST)
-    landmark = lax.psum(partial_value, "team")
+    count, landmark = (lax.axis_size("team"), partial_value)
+    for far in [1 << k for k in range(count.bit_length() - 1)]:
+        swap = [(i_2, i_2 ^ far) for i_2 in range(count)]
+        landmark = landmark + lax.ppermute(landmark, "team", swap)
     injection = jnp.einsum("scl,srl->scr", landmark, incident, precision=HIGHEST)
     driven = cotangent[0] + jnp.repeat(injection, STATES, axis=2) * obs_gain[0][None, None, :]
     offset = jnp.zeros((COLS, TEAM_STATES), jnp.float32)

time: 456 us -> 401 us (0.88)
  the two profiles are of different devices: /device:TPU:30 before, /device:TPU:6 now
where the time goes in v1:
time: 401 us; the launch traced here: 400 us
  starting transfers between devices  223 us (56%)
  waiting for transfers between devices  144 us (36%)
  matrix products  29.5 us (7%)
    ppermute x31, starting transfers between devices, from_behind(): return lax.ppermute(block, axis, route)  205 us
    ppermute x31, waiting for transfers between devices, from_behind(): return lax.ppermute(block, axis, route)  83.5 us
    ppermute x4, waiting for transfers between devices, shards(): landmark = landmark + lax.ppermute(landmark, 'team', swap)  60.2 us
    dot_general x33, matrix products, matmul(): return jnp.dot(left, right, precision=HIGHEST)  25.5 us
    ppermute x4, starting transfers between devices, shards(): landmark = landmark + lax.ppermute(landmark, 'team', swap)  17.8 us
  transfers between devices with their start and end apart: 35, of which 35 were waited for; matrix products, arithmetic and copies ran while one was open for 0% of the time, Pallas kernels for 0%

profile of v1, /device:TPU:6, one launch (start us, length us, event | category | flops | bytes accessed | tf_op | source)
XLA Modules:
  0.0 399.6 jit_solution(7567412361982550878)
XLA Ops:
  9.6 12.4 %collective-permute-done.2 = f32[1,64,2048]{2,1,0:T(8,128)S(1)} collective-permute-done((f32[1,64,2048]{2,1,0:T(8,128)S(1)}, f32[1,64,2048]{2,1,0:T(8,128)S(1)}, u32[]{:S(2)}, u32[]{:S(2)}) %collective-permute-start.2) | collective-permute-done | bytes 524320 | tf_op jit(solution)/shard_map/ppermute | solution.py:30
  26.7 22.6 %collective-permute-done.3 = f32[1,64,2048]{2,1,0:T(8,128)S(1)} collective-permute-done((f32[1,64,2048]{2,1,0:T(8,128)S(1)}, f32[1,64,2048]{2,1,0:T(8,128)S(1)}, u32[]{:S(2)}, u32[]{:S(2)}) %collective-permute-start.3) | collective-permute-done | bytes 524320 | tf_op jit(solution)/shard_map/ppermute | solution.py:30
  49.4 7.7 %collective-permute-start.4 = (f32[1,64,2048]{2,1,0:T(8,128)S(1)}, f32[1,64,2048]{2,1,0:T(8,128)S(1)}, u32[]{:S(2)}, u32[]{:S(2)}) collective-permute-start(f32[1,64,2048]{2,1,0:T(8,128)S(1)} %add.35), channel_id=1, source_target_pairs={{0,256},{32,288},{64,320},{96,352},{128,384},{160,416},{192,448},{... | collective-permute-start | bytes 1572872 | tf_op jit(solution)/shard_map/ppermute | solution.py:30
  57.2 23.3 %collective-permute-done.4 = f32[1,64,2048]{2,1,0:T(8,128)S(1)} collective-permute-done((f32[1,64,2048]{2,1,0:T(8,128)S(1)}, f32[1,64,2048]{2,1,0:T(8,128)S(1)}, u32[]{:S(2)}, u32[]{:S(2)}) %collective-permute-start.4) | collective-permute-done | bytes 524320 | tf_op jit(solution)/shard_map/ppermute | solution.py:30
  82.8 313.6 %while.10 = (s32[]{:T(128)}, f32[64,512]{1,0:T(8,128)S(1)}, f32[1,1,512,512]{3,2,1,0:T(8,128)S(1)}, f32[64,512]{1,0:T(8,128)S(1)}, f32[64,512]{1,0:T(8,128)S(1)}, /*index=5*/s32[]{:T(128)}) while((s32[]{:T(128)}, f32[64,512]{1,0:T(8,128)S(1)}, f32[1,1,512,512]{3,2,1,0:T(8,128)S(1)}, f32[64,512]{1,0:T(8,128)S(1)}, f32[64,512]{1,0:T(8,128)S(1)}, ...), condition=%wide.region_1.2_spmd, body=%wide.region_0.1_spmd.sunk | while | flops 201392128 | bytes 2359405 | solution.py:45
  83.5 11.2 %collective-permute-start = (f32[64,512]{1,0:T(8,128)S(1)}, f32[64,512]{1,0:T(8,128)S(1)}, u32[]{:S(2)}, u32[]{:S(2)}) collective-permute-start(f32[64,512]{1,0:T(8,128)S(1)} %convolution_add_fusion.4), channel_id=1, source_target_pairs={{1,0},{2,1},{3,2},{4,3},{5,4},{6,5},{7,6},{8,7},{9,8},{10,9},{11,1... | collective-permute-start | bytes 393224 | tf_op jit(solution)/shard_map/while/body/eval_jaxpr/ppermute | solution.py:15
  98.0 6.5 %collective-permute-start = (f32[64,512]{1,0:T(8,128)S(1)}, f32[64,512]{1,0:T(8,128)S(1)}, u32[]{:S(2)}, u32[]{:S(2)}) collective-permute-start(f32[64,512]{1,0:T(8,128)S(1)} %convolution_add_fusion.4), channel_id=1, source_target_pairs={{1,0},{2,1},{3,2},{4,3},{5,4},{6,5},{7,6},{8,7},{9,8},{10,9},{11,1... | collective-permute-start | bytes 393224 | tf_op jit(solution)/shard_map/while/body/eval_jaxpr/ppermute | solution.py:15
  107.8 6.5 %collective-permute-start = (f32[64,512]{1,0:T(8,128)S(1)}, f32[64,512]{1,0:T(8,128)S(1)}, u32[]{:S(2)}, u32[]{:S(2)}) collective-permute-start(f32[64,512]{1,0:T(8,128)S(1)} %convolution_add_fusion.4), channel_id=1, source_target_pairs={{1,0},{2,1},{3,2},{4,3},{5,4},{6,5},{7,6},{8,7},{9,8},{10,9},{11,1... | collective-permute-start | bytes 393224 | tf_op jit(solution)/shard_map/while/body/eval_jaxpr/ppermute | solution.py:15
  127.3 6.5 %collective-permute-start = (f32[64,512]{1,0:T(8,128)S(1)}, f32[64,512]{1,0:T(8,128)S(1)}, u32[]{:S(2)}, u32[]{:S(2)}) collective-permute-start(f32[64,512]{1,0:T(8,128)S(1)} %convolution_add_fusion.4), channel_id=1, source_target_pairs={{1,0},{2,1},{3,2},{4,3},{5,4},{6,5},{7,6},{8,7},{9,8},{10,9},{11,1... | collective-permute-start | bytes 393224 | tf_op jit(solution)/shard_map/while/body/eval_jaxpr/ppermute | solution.py:15
  137.1 6.5 %collective-permute-start = (f32[64,512]{1,0:T(8,128)S(1)}, f32[64,512]{1,0:T(8,128)S(1)}, u32[]{:S(2)}, u32[]{:S(2)}) collective-permute-start(f32[64,512]{1,0:T(8,128)S(1)} %convolution_add_fusion.4), channel_id=1, source_target_pairs={{1,0},{2,1},{3,2},{4,3},{5,4},{6,5},{7,6},{8,7},{9,8},{10,9},{11,1... | collective-permute-start | bytes 393224 | tf_op jit(solution)/shard_map/while/body/eval_jaxpr/ppermute | solution.py:15
  147.1 6.5 %collective-permute-start = (f32[64,512]{1,0:T(8,128)S(1)}, f32[64,512]{1,0:T(8,128)S(1)}, u32[]{:S(2)}, u32[]{:S(2)}) collective-permute-start(f32[64,512]{1,0:T(8,128)S(1)} %convolution_add_fusion.4), channel_id=1, source_target_pairs={{1,0},{2,1},{3,2},{4,3},{5,4},{6,5},{7,6},{8,7},{9,8},{10,9},{11,1... | collective-permute-start | bytes 393224 | tf_op jit(solution)/shard_map/while/body/eval_jaxpr/ppermute | solution.py:15
  158.2 6.5 %collective-permute-start = (f32[64,512]{1,0:T(8,128)S(1)}, f32[64,512]{1,0:T(8,128)S(1)}, u32[]{:S(2)}, u32[]{:S(2)}) collective-permute-start(f32[64,512]{1,0:T(8,128)S(1)} %convolution_add_fusion.4), channel_id=1, source_target_pairs={{1,0},{2,1},{3,2},{4,3},{5,4},{6,5},{7,6},{8,7},{9,8},{10,9},{11,1... | collective-permute-start | bytes 393224 | tf_op jit(solution)/shard_map/while/body/eval_jaxpr/ppermute | solution.py:15
  168.4 6.5 %collective-permute-start = (f32[64,512]{1,0:T(8,128)S(1)}, f32[64,512]{1,0:T(8,128)S(1)}, u32[]{:S(2)}, u32[]{:S(2)}) collective-permute-start(f32[64,512]{1,0:T(8,128)S(1)} %convolution_add_fusion.4), channel_id=1, source_target_pairs={{1,0},{2,1},{3,2},{4,3},{5,4},{6,5},{7,6},{8,7},{9,8},{10,9},{11,1... | collective-permute-start | bytes 393224 | tf_op jit(solution)/shard_map/while/body/eval_jaxpr/ppermute | solution.py:15
  188.0 6.5 %collective-permute-start = (f32[64,512]{1,0:T(8,128)S(1)}, f32[64,512]{1,0:T(8,128)S(1)}, u32[]{:S(2)}, u32[]{:S(2)}) collective-permute-start(f32[64,512]{1,0:T(8,128)S(1)} %convolution_add_fusion.4), channel_id=1, source_target_pairs={{1,0},{2,1},{3,2},{4,3},{5,4},{6,5},{7,6},{8,7},{9,8},{10,9},{11,1... | collective-permute-start | bytes 393224 | tf_op jit(solution)/shard_map/while/body/eval_jaxpr/ppermute | solution.py:15
  197.7 6.5 %collective-permute-start = (f32[64,512]{1,0:T(8,128)S(1)}, f32[64,512]{1,0:T(8,128)S(1)}, u32[]{:S(2)}, u32[]{:S(2)}) collective-permute-start(f32[64,512]{1,0:T(8,128)S(1)} %convolution_add_fusion.4), channel_id=1, source_target_pairs={{1,0},{2,1},{3,2},{4,3},{5,4},{6,5},{7,6},{8,7},{9,8},{10,9},{11,1... | collective-permute-start | bytes 393224 | tf_op jit(solution)/shard_map/while/body/eval_jaxpr/ppermute | solution.py:15
  207.5 6.5 %collective-permute-start = (f32[64,512]{1,0:T(8,128)S(1)}, f32[64,512]{1,0:T(8,128)S(1)}, u32[]{:S(2)}, u32[]{:S(2)}) collective-permute-start(f32[64,512]{1,0:T(8,128)S(1)} %convolution_add_fusion.4), channel_id=1, source_target_pairs={{1,0},{2,1},{3,2},{4,3},{5,4},{6,5},{7,6},{8,7},{9,8},{10,9},{11,1... | collective-permute-start | bytes 393224 | tf_op jit(solution)/shard_map/while/body/eval_jaxpr/ppermute | solution.py:15
  227.3 6.5 %collective-permute-start = (f32[64,512]{1,0:T(8,128)S(1)}, f32[64,512]{1,0:T(8,128)S(1)}, u32[]{:S(2)}, u32[]{:S(2)}) collective-permute-start(f32[64,512]{1,0:T(8,128)S(1)} %convolution_add_fusion.4), channel_id=1, source_target_pairs={{1,0},{2,1},{3,2},{4,3},{5,4},{6,5},{7,6},{8,7},{9,8},{10,9},{11,1... | collective-permute-start | bytes 393224 | tf_op jit(solution)/shard_map/while/body/eval_jaxpr/ppermute | solution.py:15
  238.4 6.5 %collective-permute-start = (f32[64,512]{1,0:T(8,128)S(1)}, f32[64,512]{1,0:T(8,128)S(1)}, u32[]{:S(2)}, u32[]{:S(2)}) collective-permute-start(f32[64,512]{1,0:T(8,128)S(1)} %convolution_add_fusion.4), channel_id=1, source_target_pairs={{1,0},{2,1},{3,2},{4,3},{5,4},{6,5},{7,6},{8,7},{9,8},{10,9},{11,1... | collective-permute-start | bytes 393224 | tf_op jit(solution)/shard_map/while/body/eval_jaxpr/ppermute | solution.py:15
  248.6 6.5 %collective-permute-start = (f32[64,512]{1,0:T(8,128)S(1)}, f32[64,512]{1,0:T(8,128)S(1)}, u32[]{:S(2)}, u32[]{:S(2)}) collective-permute-start(f32[64,512]{1,0:T(8,128)S(1)} %convolution_add_fusion.4), channel_id=1, source_target_pairs={{1,0},{2,1},{3,2},{4,3},{5,4},{6,5},{7,6},{8,7},{9,8},{10,9},{11,1... | collective-permute-start | bytes 393224 | tf_op jit(solution)/shard_map/while/body/eval_jaxpr/ppermute | solution.py:15
  258.4 6.5 %collective-permute-start = (f32[64,512]{1,0:T(8,128)S(1)}, f32[64,512]{1,0:T(8,128)S(1)}, u32[]{:S(2)}, u32[]{:S(2)}) collective-permute-start(f32[64,512]{1,0:T(8,128)S(1)} %convolution_add_fusion.4), channel_id=1, source_target_pairs={{1,0},{2,1},{3,2},{4,3},{5,4},{6,5},{7,6},{8,7},{9,8},{10,9},{11,1... | collective-permute-start | bytes 393224 | tf_op jit(solution)/shard_map/while/body/eval_jaxpr/ppermute | solution.py:15
  268.2 6.5 %collective-permute-start = (f32[64,512]{1,0:T(8,128)S(1)}, f32[64,512]{1,0:T(8,128)S(1)}, u32[]{:S(2)}, u32[]{:S(2)}) collective-permute-start(f32[64,512]{1,0:T(8,128)S(1)} %convolution_add_fusion.4), channel_id=1, source_target_pairs={{1,0},{2,1},{3,2},{4,3},{5,4},{6,5},{7,6},{8,7},{9,8},{10,9},{11,1... | collective-permute-start | bytes 393224 | tf_op jit(solution)/shard_map/while/body/eval_jaxpr/ppermute | solution.py:15
  277.9 6.5 %collective-permute-start = (f32[64,512]{1,0:T(8,128)S(1)}, f32[64,512]{1,0:T(8,128)S(1)}, u32[]{:S(2)}, u32[]{:S(2)}) collective-permute-start(f32[64,512]{1,0:T(8,128)S(1)} %convolution_add_fusion.4), channel_id=1, source_target_pairs={{1,0},{2,1},{3,2},{4,3},{5,4},{6,5},{7,6},{8,7},{9,8},{10,9},{11,1... | collective-permute-start | bytes 393224 | tf_op jit(solution)/shard_map/while/body/eval_jaxpr/ppermute | solution.py:15
  287.7 6.5 %collective-permute-start = (f32[64,512]{1,0:T(8,128)S(1)}, f32[64,512]{1,0:T(8,128)S(1)}, u32[]{:S(2)}, u32[]{:S(2)}) collective-permute-start(f32[64,512]{1,0:T(8,128)S(1)} %convolution_add_fusion.4), channel_id=1, source_target_pairs={{1,0},{2,1},{3,2},{4,3},{5,4},{6,5},{7,6},{8,7},{9,8},{10,9},{11,1... | collective-permute-start | bytes 393224 | tf_op jit(solution)/shard_map/while/body/eval_jaxpr/ppermute | solution.py:15
  297.4 6.5 %collective-permute-start = (f32[64,512]{1,0:T(8,128)S(1)}, f32[64,512]{1,0:T(8,128)S(1)}, u32[]{:S(2)}, u32[]{:S(2)}) collective-permute-start(f32[64,512]{1,0:T(8,128)S(1)} %convolution_add_fusion.4), channel_id=1, source_target_pairs={{1,0},{2,1},{3,2},{4,3},{5,4},{6,5},{7,6},{8,7},{9,8},{10,9},{11,1... | collective-permute-start | bytes 393224 | tf_op jit(solution)/shard_map/while/body/eval_jaxpr/ppermute | solution.py:15
  307.5 6.5 %collective-permute-start = (f32[64,512]{1,0:T(8,128)S(1)}, f32[64,512]{1,0:T(8,128)S(1)}, u32[]{:S(2)}, u32[]{:S(2)}) collective-permute-start(f32[64,512]{1,0:T(8,128)S(1)} %convolution_add_fusion.4), channel_id=1, source_target_pairs={{1,0},{2,1},{3,2},{4,3},{5,4},{6,5},{7,6},{8,7},{9,8},{10,9},{11,1... | collective-permute-start | bytes 393224 | tf_op jit(solution)/shard_map/while/body/eval_jaxpr/ppermute | solution.py:15
  318.6 6.5 %collective-permute-start = (f32[64,512]{1,0:T(8,128)S(1)}, f32[64,512]{1,0:T(8,128)S(1)}, u32[]{:S(2)}, u32[]{:S(2)}) collective-permute-start(f32[64,512]{1,0:T(8,128)S(1)} %convolution_add_fusion.4), channel_id=1, source_target_pairs={{1,0},{2,1},{3,2},{4,3},{5,4},{6,5},{7,6},{8,7},{9,8},{10,9},{11,1... | collective-permute-start | bytes 393224 | tf_op jit(solution)/shard_map/while/body/eval_jaxpr/ppermute | solution.py:15
  328.8 6.5 %collective-permute-start = (f32[64,512]{1,0:T(8,128)S(1)}, f32[64,512]{1,0:T(8,128)S(1)}, u32[]{:S(2)}, u32[]{:S(2)}) collective-permute-start(f32[64,512]{1,0:T(8,128)S(1)} %convolution_add_fusion.4), channel_id=1, source_target_pairs={{1,0},{2,1},{3,2},{4,3},{5,4},{6,5},{7,6},{8,7},{9,8},{10,9},{11,1... | collective-permute-start | bytes 393224 | tf_op jit(solution)/shard_map/while/body/eval_jaxpr/ppermute | solution.py:15
  338.6 6.5 %collective-permute-start = (f32[64,512]{1,0:T(8,128)S(1)}, f32[64,512]{1,0:T(8,128)S(1)}, u32[]{:S(2)}, u32[]{:S(2)}) collective-permute-start(f32[64,512]{1,0:T(8,128)S(1)} %convolution_add_fusion.4), channel_id=1, source_target_pairs={{1,0},{2,1},{3,2},{4,3},{5,4},{6,5},{7,6},{8,7},{9,8},{10,9},{11,1... | collective-permute-start | bytes 393224 | tf_op jit(solution)/shard_map/while/body/eval_jaxpr/ppermute | solution.py:15
  348.4 6.5 %collective-permute-start = (f32[64,512]{1,0:T(8,128)S(1)}, f32[64,512]{1,0:T(8,128)S(1)}, u32[]{:S(2)}, u32[]{:S(2)}) collective-permute-start(f32[64,512]{1,0:T(8,128)S(1)} %convolution_add_fusion.4), channel_id=1, source_target_pairs={{1,0},{2,1},{3,2},{4,3},{5,4},{6,5},{7,6},{8,7},{9,8},{10,9},{11,1... | collective-permute-start | bytes 393224 | tf_op jit(solution)/shard_map/while/body/eval_jaxpr/ppermute | solution.py:15
  358.1 6.5 %collective-permute-start = (f32[64,512]{1,0:T(8,128)S(1)}, f32[64,512]{1,0:T(8,128)S(1)}, u32[]{:S(2)}, u32[]{:S(2)}) collective-permute-start(f32[64,512]{1,0:T(8,128)S(1)} %convolution_add_fusion.4), channel_id=1, source_target_pairs={{1,0},{2,1},{3,2},{4,3},{5,4},{6,5},{7,6},{8,7},{9,8},{10,9},{11,1... | collective-permute-start | bytes 393224 | tf_op jit(solution)/shard_map/while/body/eval_jaxpr/ppermute | solution.py:15
  367.9 6.5 %collective-permute-start = (f32[64,512]{1,0:T(8,128)S(1)}, f32[64,512]{1,0:T(8,128)S(1)}, u32[]{:S(2)}, u32[]{:S(2)}) collective-permute-start(f32[64,512]{1,0:T(8,128)S(1)} %convolution_add_fusion.4), channel_id=1, source_target_pairs={{1,0},{2,1},{3,2},{4,3},{5,4},{6,5},{7,6},{8,7},{9,8},{10,9},{11,1... | collective-permute-start | bytes 393224 | tf_op jit(solution)/shard_map/while/body/eval_jaxpr/ppermute | solution.py:15
  387.4 6.5 %collective-permute-start = (f32[64,512]{1,0:T(8,128)S(1)}, f32[64,512]{1,0:T(8,128)S(1)}, u32[]{:S(2)}, u32[]{:S(2)}) collective-permute-start(f32[64,512]{1,0:T(8,128)S(1)} %convolution_add_fusion.4), channel_id=1, source_target_pairs={{1,0},{2,1},{3,2},{4,3},{5,4},{6,5},{7,6},{8,7},{9,8},{10,9},{11,1... | collective-permute-start | bytes 393224 | tf_op jit(solution)/shard_map/while/body/eval_jaxpr/ppermute | solution.py:15
  (125 shorter events, 152.5 us)
Async XLA Ops:
  6.1 15.9 %collective-permute-start.2 = (f32[1,64,2048]{2,1,0:T(8,128)S(1)}, f32[1,64,2048]{2,1,0:T(8,128)S(1)}, u32[]{:S(2)}, u32[]{:S(2)}) collective-permute-start(f32[1,64,2048]{2,1,0:T(8,128)S(1)} %add.33), channel_id=1, source_target_pairs={{0,64},{32,96},{64,0},{96,32},{128,192},{160,224},{192,128},{224,1... | collective-permute-start | bytes 1572872 | tf_op jit(solution)/shard_map/ppermute | solution.py:30
  22.1 27.3 %collective-permute-start.3 = (f32[1,64,2048]{2,1,0:T(8,128)S(1)}, f32[1,64,2048]{2,1,0:T(8,128)S(1)}, u32[]{:S(2)}, u32[]{:S(2)}) collective-permute-start(f32[1,64,2048]{2,1,0:T(8,128)S(1)} %add.34), channel_id=1, source_target_pairs={{0,128},{32,160},{64,192},{96,224},{128,0},{160,32},{192,64},{224,... | collective-permute-start | bytes 1572872 | tf_op jit(solution)/shard_map/ppermute | solution.py:30
  49.4 31.1 %collective-permute-start.4 = (f32[1,64,2048]{2,1,0:T(8,128)S(1)}, f32[1,64,2048]{2,1,0:T(8,128)S(1)}, u32[]{:S(2)}, u32[]{:S(2)}) collective-permute-start(f32[1,64,2048]{2,1,0:T(8,128)S(1)} %add.35), channel_id=1, source_target_pairs={{0,256},{32,288},{64,320},{96,352},{128,384},{160,416},{192,448},{... | collective-permute-start | bytes 1572872 | tf_op jit(solution)/shard_map/ppermute | solution.py:30
  83.5 13.7 %collective-permute-start = (f32[64,512]{1,0:T(8,128)S(1)}, f32[64,512]{1,0:T(8,128)S(1)}, u32[]{:S(2)}, u32[]{:S(2)}) collective-permute-start(f32[64,512]{1,0:T(8,128)S(1)} %convolution_add_fusion.4), channel_id=1, source_target_pairs={{1,0},{2,1},{3,2},{4,3},{5,4},{6,5},{7,6},{8,7},{9,8},{10,9},{11,1... | collective-permute-start | bytes 393224 | tf_op jit(solution)/shard_map/while/body/eval_jaxpr/ppermute | solution.py:15
  98.0 9.0 %collective-permute-start = (f32[64,512]{1,0:T(8,128)S(1)}, f32[64,512]{1,0:T(8,128)S(1)}, u32[]{:S(2)}, u32[]{:S(2)}) collective-permute-start(f32[64,512]{1,0:T(8,128)S(1)} %convolution_add_fusion.4), channel_id=1, source_target_pairs={{1,0},{2,1},{3,2},{4,3},{5,4},{6,5},{7,6},{8,7},{9,8},{10,9},{11,1... | collective-permute-start | bytes 393224 | tf_op jit(solution)/shard_map/while/body/eval_jaxpr/ppermute | solution.py:15
  107.8 9.0 %collective-permute-start = (f32[64,512]{1,0:T(8,128)S(1)}, f32[64,512]{1,0:T(8,128)S(1)}, u32[]{:S(2)}, u32[]{:S(2)}) collective-permute-start(f32[64,512]{1,0:T(8,128)S(1)} %convolution_add_fusion.4), channel_id=1, source_target_pairs={{1,0},{2,1},{3,2},{4,3},{5,4},{6,5},{7,6},{8,7},{9,8},{10,9},{11,1... | collective-permute-start | bytes 393224 | tf_op jit(solution)/shard_map/while/body/eval_jaxpr/ppermute | solution.py:15
  117.6 9.0 %collective-permute-start = (f32[64,512]{1,0:T(8,128)S(1)}, f32[64,512]{1,0:T(8,128)S(1)}, u32[]{:S(2)}, u32[]{:S(2)}) collective-permute-start(f32[64,512]{1,0:T(8,128)S(1)} %convolution_add_fusion.4), channel_id=1, source_target_pairs={{1,0},{2,1},{3,2},{4,3},{5,4},{6,5},{7,6},{8,7},{9,8},{10,9},{11,1... | collective-permute-start | bytes 393224 | tf_op jit(solution)/shard_map/while/body/eval_jaxpr/ppermute | solution.py:15
  127.3 9.0 %collective-permute-start = (f32[64,512]{1,0:T(8,128)S(1)}, f32[64,512]{1,0:T(8,128)S(1)}, u32[]{:S(2)}, u32[]{:S(2)}) collective-permute-start(f32[64,512]{1,0:T(8,128)S(1)} %convolution_add_fusion.4), channel_id=1, source_target_pairs={{1,0},{2,1},{3,2},{4,3},{5,4},{6,5},{7,6},{8,7},{9,8},{10,9},{11,1... | collective-permute-start | bytes 393224 | tf_op jit(solution)/shard_map/while/body/eval_jaxpr/ppermute | solution.py:15
  137.1 9.3 %collective-permute-start = (f32[64,512]{1,0:T(8,128)S(1)}, f32[64,512]{1,0:T(8,128)S(1)}, u32[]{:S(2)}, u32[]{:S(2)}) collective-permute-start(f32[64,512]{1,0:T(8,128)S(1)} %convolution_add_fusion.4), channel_id=1, source_target_pairs={{1,0},{2,1},{3,2},{4,3},{5,4},{6,5},{7,6},{8,7},{9,8},{10,9},{11,1... | collective-permute-start | bytes 393224 | tf_op jit(solution)/shard_map/while/body/eval_jaxpr/ppermute | solution.py:15
  147.1 10.3 %collective-permute-start = (f32[64,512]{1,0:T(8,128)S(1)}, f32[64,512]{1,0:T(8,128)S(1)}, u32[]{:S(2)}, u32[]{:S(2)}) collective-permute-start(f32[64,512]{1,0:T(8,128)S(1)} %convolution_add_fusion.4), channel_id=1, source_target_pairs={{1,0},{2,1},{3,2},{4,3},{5,4},{6,5},{7,6},{8,7},{9,8},{10,9},{11,1... | collective-permute-start | bytes 393224 | tf_op jit(solution)/shard_map/while/body/eval_jaxpr/ppermute | solution.py:15
  158.2 9.4 %collective-permute-start = (f32[64,512]{1,0:T(8,128)S(1)}, f32[64,512]{1,0:T(8,128)S(1)}, u32[]{:S(2)}, u32[]{:S(2)}) collective-permute-start(f32[64,512]{1,0:T(8,128)S(1)} %convolution_add_fusion.4), channel_id=1, source_target_pairs={{1,0},{2,1},{3,2},{4,3},{5,4},{6,5},{7,6},{8,7},{9,8},{10,9},{11,1... | collective-permute-start | bytes 393224 | tf_op jit(solution)/shard_map/while/body/eval_jaxpr/ppermute | solution.py:15
  168.4 9.0 %collective-permute-start = (f32[64,512]{1,0:T(8,128)S(1)}, f32[64,512]{1,0:T(8,128)S(1)}, u32[]{:S(2)}, u32[]{:S(2)}) collective-permute-start(f32[64,512]{1,0:T(8,128)S(1)} %convolution_add_fusion.4), channel_id=1, source_target_pairs={{1,0},{2,1},{3,2},{4,3},{5,4},{6,5},{7,6},{8,7},{9,8},{10,9},{11,1... | collective-permute-start | bytes 393224 | tf_op jit(solution)/shard_map/while/body/eval_jaxpr/ppermute | solution.py:15
  178.2 9.0 %collective-permute-start = (f32[64,512]{1,0:T(8,128)S(1)}, f32[64,512]{1,0:T(8,128)S(1)}, u32[]{:S(2)}, u32[]{:S(2)}) collective-permute-start(f32[64,512]{1,0:T(8,128)S(1)} %convolution_add_fusion.4), channel_id=1, source_target_pairs={{1,0},{2,1},{3,2},{4,3},{5,4},{6,5},{7,6},{8,7},{9,8},{10,9},{11,1... | collective-permute-start | bytes 393224 | tf_op jit(solution)/shard_map/while/body/eval_jaxpr/ppermute | solution.py:15
  188.0 9.0 %collective-permute-start = (f32[64,512]{1,0:T(8,128)S(1)}, f32[64,512]{1,0:T(8,128)S(1)}, u32[]{:S(2)}, u32[]{:S(2)}) collective-permute-start(f32[64,512]{1,0:T(8,128)S(1)} %convolution_add_fusion.4), channel_id=1, source_target_pairs={{1,0},{2,1},{3,2},{4,3},{5,4},{6,5},{7,6},{8,7},{9,8},{10,9},{11,1... | collective-permute-start | bytes 393224 | tf_op jit(solution)/shard_map/while/body/eval_jaxpr/ppermute | solution.py:15
  197.7 9.0 %collective-permute-start = (f32[64,512]{1,0:T(8,128)S(1)}, f32[64,512]{1,0:T(8,128)S(1)}, u32[]{:S(2)}, u32[]{:S(2)}) collective-permute-start(f32[64,512]{1,0:T(8,128)S(1)} %convolution_add_fusion.4), channel_id=1, source_target_pairs={{1,0},{2,1},{3,2},{4,3},{5,4},{6,5},{7,6},{8,7},{9,8},{10,9},{11,1... | collective-permute-start | bytes 393224 | tf_op jit(solution)/shard_map/while/body/eval_jaxpr/ppermute | solution.py:15
  207.5 9.0 %collective-permute-start = (f32[64,512]{1,0:T(8,128)S(1)}, f32[64,512]{1,0:T(8,128)S(1)}, u32[]{:S(2)}, u32[]{:S(2)}) collective-permute-start(f32[64,512]{1,0:T(8,128)S(1)} %convolution_add_fusion.4), channel_id=1, source_target_pairs={{1,0},{2,1},{3,2},{4,3},{5,4},{6,5},{7,6},{8,7},{9,8},{10,9},{11,1... | collective-permute-start | bytes 393224 | tf_op jit(solution)/shard_map/while/body/eval_jaxpr/ppermute | solution.py:15
  217.3 9.3 %collective-permute-start = (f32[64,512]{1,0:T(8,128)S(1)}, f32[64,512]{1,0:T(8,128)S(1)}, u32[]{:S(2)}, u32[]{:S(2)}) collective-permute-start(f32[64,512]{1,0:T(8,128)S(1)} %convolution_add_fusion.4), channel_id=1, source_target_pairs={{1,0},{2,1},{3,2},{4,3},{5,4},{6,5},{7,6},{8,7},{9,8},{10,9},{11,1... | collective-permute-start | bytes 393224 | tf_op jit(solution)/shard_map/while/body/eval_jaxpr/ppermute | solution.py:15
  227.3 10.3 %collective-permute-start = (f32[64,512]{1,0:T(8,128)S(1)}, f32[64,512]{1,0:T(8,128)S(1)}, u32[]{:S(2)}, u32[]{:S(2)}) collective-permute-start(f32[64,512]{1,0:T(8,128)S(1)} %convolution_add_fusion.4), channel_id=1, source_target_pairs={{1,0},{2,1},{3,2},{4,3},{5,4},{6,5},{7,6},{8,7},{9,8},{10,9},{11,1... | collective-permute-start | bytes 393224 | tf_op jit(solution)/shard_map/while/body/eval_jaxpr/ppermute | solution.py:15
  238.4 9.4 %collective-permute-start = (f32[64,512]{1,0:T(8,128)S(1)}, f32[64,512]{1,0:T(8,128)S(1)}, u32[]{:S(2)}, u32[]{:S(2)}) collective-permute-start(f32[64,512]{1,0:T(8,128)S(1)} %convolution_add_fusion.4), channel_id=1, source_target_pairs={{1,0},{2,1},{3,2},{4,3},{5,4},{6,5},{7,6},{8,7},{9,8},{10,9},{11,1... | collective-permute-start | bytes 393224 | tf_op jit(solution)/shard_map/while/body/eval_jaxpr/ppermute | solution.py:15
  248.6 9.0 %collective-permute-start = (f32[64,512]{1,0:T(8,128)S(1)}, f32[64,512]{1,0:T(8,128)S(1)}, u32[]{:S(2)}, u32[]{:S(2)}) collective-permute-start(f32[64,512]{1,0:T(8,128)S(1)} %convolution_add_fusion.4), channel_id=1, source_target_pairs={{1,0},{2,1},{3,2},{4,3},{5,4},{6,5},{7,6},{8,7},{9,8},{10,9},{11,1... | collective-permute-start | bytes 393224 | tf_op jit(solution)/shard_map/while/body/eval_jaxpr/ppermute | solution.py:15
  258.4 9.0 %collective-permute-start = (f32[64,512]{1,0:T(8,128)S(1)}, f32[64,512]{1,0:T(8,128)S(1)}, u32[]{:S(2)}, u32[]{:S(2)}) collective-permute-start(f32[64,512]{1,0:T(8,128)S(1)} %convolution_add_fusion.4), channel_id=1, source_target_pairs={{1,0},{2,1},{3,2},{4,3},{5,4},{6,5},{7,6},{8,7},{9,8},{10,9},{11,1... | collective-permute-start | bytes 393224 | tf_op jit(solution)/shard_map/while/body/eval_jaxpr/ppermute | solution.py:15
  268.2 9.0 %collective-permute-start = (f32[64,512]{1,0:T(8,128)S(1)}, f32[64,512]{1,0:T(8,128)S(1)}, u32[]{:S(2)}, u32[]{:S(2)}) collective-permute-start(f32[64,512]{1,0:T(8,128)S(1)} %convolution_add_fusion.4), channel_id=1, source_target_pairs={{1,0},{2,1},{3,2},{4,3},{5,4},{6,5},{7,6},{8,7},{9,8},{10,9},{11,1... | collective-permute-start | bytes 393224 | tf_op jit(solution)/shard_map/while/body/eval_jaxpr/ppermute | solution.py:15
  277.9 9.0 %collective-permute-start = (f32[64,512]{1,0:T(8,128)S(1)}, f32[64,512]{1,0:T(8,128)S(1)}, u32[]{:S(2)}, u32[]{:S(2)}) collective-permute-start(f32[64,512]{1,0:T(8,128)S(1)} %convolution_add_fusion.4), channel_id=1, source_target_pairs={{1,0},{2,1},{3,2},{4,3},{5,4},{6,5},{7,6},{8,7},{9,8},{10,9},{11,1... | collective-permute-start | bytes 393224 | tf_op jit(solution)/shard_map/while/body/eval_jaxpr/ppermute | solution.py:15
  287.7 9.0 %collective-permute-start = (f32[64,512]{1,0:T(8,128)S(1)}, f32[64,512]{1,0:T(8,128)S(1)}, u32[]{:S(2)}, u32[]{:S(2)}) collective-permute-start(f32[64,512]{1,0:T(8,128)S(1)} %convolution_add_fusion.4), channel_id=1, source_target_pairs={{1,0},{2,1},{3,2},{4,3},{5,4},{6,5},{7,6},{8,7},{9,8},{10,9},{11,1... | collective-permute-start | bytes 393224 | tf_op jit(solution)/shard_map/while/body/eval_jaxpr/ppermute | solution.py:15
  297.4 9.3 %collective-permute-start = (f32[64,512]{1,0:T(8,128)S(1)}, f32[64,512]{1,0:T(8,128)S(1)}, u32[]{:S(2)}, u32[]{:S(2)}) collective-permute-start(f32[64,512]{1,0:T(8,128)S(1)} %convolution_add_fusion.4), channel_id=1, source_target_pairs={{1,0},{2,1},{3,2},{4,3},{5,4},{6,5},{7,6},{8,7},{9,8},{10,9},{11,1... | collective-permute-start | bytes 393224 | tf_op jit(solution)/shard_map/while/body/eval_jaxpr/ppermute | solution.py:15
  307.5 10.3 %collective-permute-start = (f32[64,512]{1,0:T(8,128)S(1)}, f32[64,512]{1,0:T(8,128)S(1)}, u32[]{:S(2)}, u32[]{:S(2)}) collective-permute-start(f32[64,512]{1,0:T(8,128)S(1)} %convolution_add_fusion.4), channel_id=1, source_target_pairs={{1,0},{2,1},{3,2},{4,3},{5,4},{6,5},{7,6},{8,7},{9,8},{10,9},{11,1... | collective-permute-start | bytes 393224 | tf_op jit(solution)/shard_map/while/body/eval_jaxpr/ppermute | solution.py:15
  318.6 9.4 %collective-permute-start = (f32[64,512]{1,0:T(8,128)S(1)}, f32[64,512]{1,0:T(8,128)S(1)}, u32[]{:S(2)}, u32[]{:S(2)}) collective-permute-start(f32[64,512]{1,0:T(8,128)S(1)} %convolution_add_fusion.4), channel_id=1, source_target_pairs={{1,0},{2,1},{3,2},{4,3},{5,4},{6,5},{7,6},{8,7},{9,8},{10,9},{11,1... | collective-permute-start | bytes 393224 | tf_op jit(solution)/shard_map/while/body/eval_jaxpr/ppermute | solution.py:15
  328.8 9.0 %collective-permute-start = (f32[64,512]{1,0:T(8,128)S(1)}, f32[64,512]{1,0:T(8,128)S(1)}, u32[]{:S(2)}, u32[]{:S(2)}) collective-permute-start(f32[64,512]{1,0:T(8,128)S(1)} %convolution_add_fusion.4), channel_id=1, source_target_pairs={{1,0},{2,1},{3,2},{4,3},{5,4},{6,5},{7,6},{8,7},{9,8},{10,9},{11,1... | collective-permute-start | bytes 393224 | tf_op jit(solution)/shard_map/while/body/eval_jaxpr/ppermute | solution.py:15
  338.6 9.0 %collective-permute-start = (f32[64,512]{1,0:T(8,128)S(1)}, f32[64,512]{1,0:T(8,128)S(1)}, u32[]{:S(2)}, u32[]{:S(2)}) collective-permute-start(f32[64,512]{1,0:T(8,128)S(1)} %convolution_add_fusion.4), channel_id=1, source_target_pairs={{1,0},{2,1},{3,2},{4,3},{5,4},{6,5},{7,6},{8,7},{9,8},{10,9},{11,1... | collective-permute-start | bytes 393224 | tf_op jit(solution)/shard_map/while/body/eval_jaxpr/ppermute | solution.py:15
  348.4 9.0 %collective-permute-start = (f32[64,512]{1,0:T(8,128)S(1)}, f32[64,512]{1,0:T(8,128)S(1)}, u32[]{:S(2)}, u32[]{:S(2)}) collective-permute-start(f32[64,512]{1,0:T(8,128)S(1)} %convolution_add_fusion.4), channel_id=1, source_target_pairs={{1,0},{2,1},{3,2},{4,3},{5,4},{6,5},{7,6},{8,7},{9,8},{10,9},{11,1... | collective-permute-start | bytes 393224 | tf_op jit(solution)/shard_map/while/body/eval_jaxpr/ppermute | solution.py:15
  358.1 9.0 %collective-permute-start = (f32[64,512]{1,0:T(8,128)S(1)}, f32[64,512]{1,0:T(8,128)S(1)}, u32[]{:S(2)}, u32[]{:S(2)}) collective-permute-start(f32[64,512]{1,0:T(8,128)S(1)} %convolution_add_fusion.4), channel_id=1, source_target_pairs={{1,0},{2,1},{3,2},{4,3},{5,4},{6,5},{7,6},{8,7},{9,8},{10,9},{11,1... | collective-permute-start | bytes 393224 | tf_op jit(solution)/shard_map/while/body/eval_jaxpr/ppermute | solution.py:15
  387.4 9.0 %collective-permute-start = (f32[64,512]{1,0:T(8,128)S(1)}, f32[64,512]{1,0:T(8,128)S(1)}, u32[]{:S(2)}, u32[]{:S(2)}) collective-permute-start(f32[64,512]{1,0:T(8,128)S(1)} %convolution_add_fusion.4), channel_id=1, source_target_pairs={{1,0},{2,1},{3,2},{4,3},{5,4},{6,5},{7,6},{8,7},{9,8},{10,9},{11,1... | collective-permute-start | bytes 393224 | tf_op jit(solution)/shard_map/while/body/eval_jaxpr/ppermute | solution.py:15
  (9 other events, 503.2 us)
